TPU v7x, 32 devices: a whole 2x2x4 slice. The times are simulated.
32 devices in a mesh: dp: 8 (over y, x, core), tensor: 4 (over z).
Axes of the slice: x: 2, y: 2, z: 4, core: 2. Of those that a mesh axis runs over, the one named last changes fastest.
Arguments:
- tokens: bfloat16 [20480, 768], P(('dp', 'tensor')), may hold values from -6 to 6
- visible_counts: int32 [256], P('dp'), may hold values from 20 to 78, as said below
- norm_one_gain: float32 [768], replicated, may hold values from 0.1 to 1.9
- norm_one_shift: float32 [768], replicated, may hold values from -1.8 to 1.8
- input_weight: bfloat16 [768, 3, 768], P(None, None, 'tensor'), may hold values from -0.21875 to 0.21875
- input_bias: bfloat16 [2, 768], P(None, 'tensor'), may hold values from -1.796875 to 1.796875
- mixer_weight: bfloat16 [768, 768], P('tensor'), may hold values from -1.25 to 1.25
- mixer_bias: float32 [768], replicated, may hold values from -1.8 to 1.8
- norm_two_gain: float32 [768], replicated, may hold values from 0.1 to 1.9
- norm_two_shift: float32 [768], replicated, may hold values from -1.8 to 1.8
- up_weight: bfloat16 [768, 3072], P(None, 'tensor'), may hold values from -0.21875 to 0.21875
- up_bias: bfloat16 [3072], P('tensor'), may hold values from -1.796875 to 1.796875
- down_weight: bfloat16 [3072, 768], P('tensor'), may hold values from -0.109375 to 0.109375
- down_bias: float32 [768], replicated, may hold values from -1.8 to 1.8
- output_grad: bfloat16 [20480, 768], P(('dp', 'tensor')), may hold values from -6 to 6
Outputs:
- block_output: bfloat16 [20480, 768], P(('dp', 'tensor'))
- grad_tokens: float32 [20480, 768], P(('dp', 'tensor'))
- grad_norm_one_gain: float32 [768], replicated
- grad_norm_one_shift: float32 [768], replicated
- grad_input_weight: float32 [768, 3, 768], P(None, None, 'tensor')
- grad_input_bias: float32 [2, 768], P(None, 'tensor')
- grad_mixer_weight: float32 [768, 768], P('tensor')
- grad_mixer_bias: float32 [768], replicated
- grad_norm_two_gain: float32 [768], replicated
- grad_norm_two_shift: float32 [768], replicated
- grad_up_weight: float32 [768, 3072], P(None, 'tensor')
- grad_up_bias: float32 [3072], P('tensor')
- grad_down_weight: float32 [3072, 768], P('tensor')
- grad_down_bias: float32 [768], replicated
Inputs may be any that keep to these rules, and one draw needn't show every extreme that they name: `visible_counts`: each image has 20 to 78 visible patches; some image has exactly 78 and some exactly 20.
All inputs are finite; a program needn't handle non-finite values.
Results may differ from a plain program's by a relative error of at most 0.014.
Values may be sent and summed in bfloat16 or wider, within the bound.
No kernel may reach another device: no remote copies, remote signals or barrier semaphores. Data moves between devices by JAX's collectives and lax.ppermute only.
A program may use at most 128 MiB of HBM per device.

v0:
```python
import jax
import jax.numpy as jnp
from jax import lax
from jax.sharding import PartitionSpec as P

HD = 64
SLOTS = 80
masked_score = -1000000000.0


def layer_norm(inputs, norm_gain, norm_shift):
    center = inputs - jnp.mean(inputs, axis=-1, keepdims=True)
    spread = jnp.mean(center * center, axis=-1, keepdims=True)
    return center * lax.rsqrt(spread + 1e-06) * norm_gain + norm_shift


def norm_back(inputs, norm_gain, norm_shift, grad_normed):
    unused, pullback = jax.vjp(layer_norm, inputs, norm_gain, norm_shift)
    return pullback(grad_normed)


def gelu_exact(inputs):
    return jax.nn.gelu(inputs, approximate=False)


def split_heads(flat, slot_count, head_dim):
    return flat.reshape(
        flat.shape[0] // slot_count, slot_count, flat.shape[1] // head_dim, head_dim
    )


def visible_keys(counts, slot_count):
    return (lax.broadcasted_iota(jnp.int32, (counts.shape[0], slot_count), 1) < counts[:, None])[
        :, None, None, :
    ]


def project_inputs(normed_rows, weight_in, bias_in, slot_count, head_dim):
    columns = weight_in.shape[2]
    product = jnp.dot(
        normed_rows,
        weight_in.reshape(weight_in.shape[0], 3 * columns),
        preferred_element_type=jnp.float32,
    ).reshape(-1, 3, columns)
    queries = (product[:, 0] + bias_in[0]).astype(jnp.bfloat16)
    key_rows = product[:, 1].astype(jnp.bfloat16)
    values = (product[:, 2] + bias_in[1]).astype(jnp.bfloat16)
    return (
        split_heads(queries, slot_count, head_dim),
        split_heads(key_rows, slot_count, head_dim),
        split_heads(values, slot_count, head_dim),
    )


def attend(queries, key_rows, values, counts):
    factor = queries.shape[-1] ** (-0.5)
    scores = (
        jnp.einsum("bqhd,bkhd->bhqk", queries, key_rows, preferred_element_type=jnp.float32)
        * factor
    )
    scores = jnp.where(visible_keys(counts, key_rows.shape[1]), scores, masked_score)
    maxima = jnp.max(scores, axis=-1, keepdims=True)
    exponent = jnp.exp(scores - maxima)
    totals = jnp.sum(exponent, axis=-1, keepdims=True)
    soft_low = (exponent / totals).astype(jnp.bfloat16)
    blended = jnp.einsum("bhqk,bkhd->bqhd", soft_low, values, preferred_element_type=jnp.float32)
    return (blended, maxima + jnp.log(totals))


def attend_back(queries, key_rows, values, counts, log_totals, grad_blend):
    factor = queries.shape[-1] ** (-0.5)
    scores = (
        jnp.einsum("bqhd,bkhd->bhqk", queries, key_rows, preferred_element_type=jnp.float32)
        * factor
    )
    scores = jnp.where(visible_keys(counts, key_rows.shape[1]), scores, masked_score)
    soft = jnp.exp(scores - log_totals)
    soft_low = soft.astype(jnp.bfloat16)
    grad_values = jnp.einsum(
        "bhqk,bqhd->bkhd", soft_low, grad_blend, preferred_element_type=jnp.float32
    )
    grad_soft = jnp.einsum(
        "bqhd,bkhd->bhqk", grad_blend, values, preferred_element_type=jnp.float32
    )
    grad_scores = soft * (grad_soft - jnp.sum(grad_soft * soft, axis=-1, keepdims=True))
    grad_low = grad_scores.astype(jnp.bfloat16)
    grad_queries = (
        jnp.einsum("bhqk,bkhd->bqhd", grad_low, key_rows, preferred_element_type=jnp.float32)
        * factor
    )
    grad_keys = (
        jnp.einsum("bhqk,bqhd->bkhd", grad_low, queries, preferred_element_type=jnp.float32)
        * factor
    )
    return (grad_queries, grad_keys, grad_values)


def mlp_back(normed_rows, hidden_pre, active, grad_rows, weight_down):
    grad_down = jnp.einsum("rf,rd->fd", active, grad_rows, preferred_element_type=jnp.float32)
    grad_active = jnp.einsum(
        "rd,fd->rf", grad_rows, weight_down, preferred_element_type=jnp.float32
    )
    unused, pullback = jax.vjp(gelu_exact, hidden_pre)
    grad_pre = pullback(grad_active)[0]
    grad_up_b = jnp.sum(grad_pre, axis=0)
    grad_pre_low = grad_pre.astype(jnp.bfloat16)
    grad_up = jnp.einsum("rd,rf->df", normed_rows, grad_pre_low, preferred_element_type=jnp.float32)
    return (grad_down, grad_up, grad_up_b, grad_pre_low)


def mixer_back(
    normed_rows,
    queries,
    key_rows,
    values,
    counts,
    log_totals,
    grad_rows,
    blend_low,
    weight_mix,
    slot_count,
    head_dim,
):
    row_total = blend_low.shape[0]
    grad_mix = jnp.einsum("rc,rd->cd", blend_low, grad_rows, preferred_element_type=jnp.float32)
    grad_blend = jnp.einsum(
        "rd,cd->rc", grad_rows, weight_mix, preferred_element_type=jnp.float32
    ).astype(jnp.bfloat16)
    grad_queries, grad_keys, grad_values = attend_back(
        queries, key_rows, values, counts, log_totals, split_heads(grad_blend, slot_count, head_dim)
    )
    grad_queries = grad_queries.reshape(row_total, -1)
    grad_keys = grad_keys.reshape(row_total, -1)
    grad_values = grad_values.reshape(row_total, -1)
    grad_bias_in = jnp.stack([jnp.sum(grad_queries, axis=0), jnp.sum(grad_values, axis=0)])
    grad_projected = jnp.stack([grad_queries, grad_keys, grad_values], axis=1).astype(jnp.bfloat16)
    grad_weight_in = jnp.einsum(
        "rd,rjc->djc", normed_rows, grad_projected, preferred_element_type=jnp.float32
    )
    return (grad_mix, grad_bias_in, grad_weight_in, grad_projected)


def local(
    tokens,
    visible_counts,
    norm_one_gain,
    norm_one_shift,
    input_weight,
    input_bias,
    mixer_weight,
    mixer_bias,
    norm_two_gain,
    norm_two_shift,
    up_weight,
    up_bias,
    down_weight,
    down_bias,
    output_grad,
):
    slot_count = SLOTS
    head_dim = HD
    inputs = tokens.astype(jnp.float32)
    grad_output = output_grad.astype(jnp.float32)
    low_one = layer_norm(inputs, norm_one_gain, norm_one_shift).astype(jnp.bfloat16)
    whole_one = lax.all_gather(low_one, "tensor", axis=0, tiled=True)
    queries, key_rows, values = project_inputs(
        whole_one, input_weight, input_bias, slot_count, head_dim
    )
    blended, log_totals = attend(queries, key_rows, values, visible_counts)
    blend_low = blended.reshape(whole_one.shape[0], -1).astype(jnp.bfloat16)
    first_sum = (
        inputs
        + lax.psum_scatter(
            jnp.dot(blend_low, mixer_weight, preferred_element_type=jnp.float32),
            "tensor",
            scatter_dimension=0,
            tiled=True,
        )
        + mixer_bias
    )
    low_two = layer_norm(first_sum, norm_two_gain, norm_two_shift).astype(jnp.bfloat16)
    whole_two = lax.all_gather(low_two, "tensor", axis=0, tiled=True)
    hidden_pre = jnp.dot(whole_two, up_weight, preferred_element_type=jnp.float32) + up_bias
    active = gelu_exact(hidden_pre).astype(jnp.bfloat16)
    result = (
        first_sum
        + lax.psum_scatter(
            jnp.dot(active, down_weight, preferred_element_type=jnp.float32).astype(jnp.bfloat16),
            "tensor",
            scatter_dimension=0,
            tiled=True,
        ).astype(jnp.float32)
        + down_bias
    )
    whole_grad = lax.all_gather(output_grad, "tensor", axis=0, tiled=True)
    grad_down, grad_up, grad_up_b, grad_pre_low = mlp_back(
        whole_two, hidden_pre, active, whole_grad, down_weight
    )
    grad_normed_two = lax.psum_scatter(
        jnp.einsum("rf,df->rd", grad_pre_low, up_weight, preferred_element_type=jnp.float32),
        "tensor",
        scatter_dimension=0,
        tiled=True,
    )
    grad_first, grad_gain_two, grad_shift_two = norm_back(
        first_sum, norm_two_gain, norm_two_shift, grad_normed_two
    )
    grad_first = grad_output + grad_first
    whole_first = lax.all_gather(grad_first.astype(jnp.bfloat16), "tensor", axis=0, tiled=True)
    grad_mix, grad_bias_in, grad_weight_in, grad_projected = mixer_back(
        whole_one,
        queries,
        key_rows,
        values,
        visible_counts,
        log_totals,
        whole_first,
        blend_low,
        mixer_weight,
        slot_count,
        head_dim,
    )
    grad_normed_one = lax.psum_scatter(
        jnp.einsum(
            "rjc,djc->rd", grad_projected, input_weight, preferred_element_type=jnp.float32
        ).astype(jnp.bfloat16),
        "tensor",
        scatter_dimension=0,
        tiled=True,
    ).astype(jnp.float32)
    weight_terms = (grad_weight_in, grad_bias_in, grad_mix, grad_up, grad_up_b, grad_down)
    grad_inputs, grad_gain_one, grad_shift_one = norm_back(
        inputs, norm_one_gain, norm_one_shift, grad_normed_one
    )
    grad_tokens = grad_first + grad_inputs
    sum_gain_one, sum_shift_one, sum_mix_bias, sum_gain_two, sum_shift_two, sum_down_bias = (
        lax.psum(
            (
                grad_gain_one,
                grad_shift_one,
                jnp.sum(grad_first, axis=0),
                grad_gain_two,
                grad_shift_two,
                jnp.sum(grad_output, axis=0),
            ),
            ("dp", "tensor"),
        )
    )
    sum_weight_in, sum_bias_in, sum_mix, sum_up, sum_up_b, sum_down = lax.psum(
        (
            weight_terms[0],
            weight_terms[1],
            weight_terms[2],
            weight_terms[3],
            weight_terms[4],
            weight_terms[5],
        ),
        "dp",
    )
    return (
        result.astype(jnp.bfloat16),
        grad_tokens,
        sum_gain_one,
        sum_shift_one,
        sum_weight_in,
        sum_bias_in,
        sum_mix,
        sum_mix_bias,
        sum_gain_two,
        sum_shift_two,
        sum_up,
        sum_up_b,
        sum_down,
        sum_down_bias,
    )


def solution(mesh):
    in_specs = (
        P(("dp", "tensor"), None),
        P("dp"),
        P(),
        P(),
        P(None, None, "tensor"),
        P(None, "tensor"),
        P("tensor", None),
        P(),
        P(),
        P(),
        P(None, "tensor"),
        P("tensor"),
        P("tensor", None),
        P(),
        P(("dp", "tensor"), None),
    )
    out_specs = (
        P(("dp", "tensor"), None),
        P(("dp", "tensor"), None),
        P(),
        P(),
        P(None, None, "tensor"),
        P(None, "tensor"),
        P("tensor", None),
        P(),
        P(),
        P(),
        P(None, "tensor"),
        P("tensor"),
        P("tensor", None),
        P(),
    )
    return jax.shard_map(local, mesh=mesh, in_specs=in_specs, out_specs=out_specs, check_vma=False)
```

profile of v0, /device:TPU:0, one launch (start us, length us, event | category | flops | bytes accessed | tf_op | source)
XLA Modules:
  0.0 1010.1 jit_solution(16693348201039939642)
XLA Ops:
  14.6 79.0 %all-gather.5.cloned.1.call-done = bf16[2560,768]{1,0:T(8,128)(2,1)} async-done(((bf16[640,768]{1,0:T(8,128)(2,1)}), bf16[2560,768]{1,0:T(8,128)(2,1)}) %all-gather.5.cloned.1.call-update) | async-done | bytes 3932176 | tf_op jit(solution)/shard_map/all_gather | solution.py:165
  93.6 4.6 fusion.6
  104.7 4.7 squeeze.4
  113.5 5.2 fusion.57
  135.3 134.9 %reduce-scatter.5.cloned.1.call-done = f32[640,768]{1,0:T(8,128)} async-done(((f32[2560,768]{1,0:T(8,128)}), f32[640,768]{1,0:T(8,128)}) %reduce-scatter.5.cloned.1.call-update) | async-done | bytes 1966096 | tf_op jit(solution)/shard_map/reduce_scatter | solution.py:173
  274.7 76.5 %all-gather.7.cloned.1.call-done = bf16[2560,768]{1,0:T(8,128)(2,1)} async-done(((bf16[640,768]{1,0:T(8,128)(2,1)}), bf16[2560,768]{1,0:T(8,128)(2,1)}) %all-gather.7.cloned.1.call-update) | async-done | bytes 3932176 | tf_op jit(solution)/shard_map/all_gather | solution.py:182
  351.2 9.0 fusion.59
  360.2 67.5 %all-gather.9.cloned.1.call-done = bf16[2560,768]{1,0:T(8,128)(2,1)} async-done(((bf16[640,768]{1,0:T(8,128)(2,1)}), bf16[2560,768]{1,0:T(8,128)(2,1)}) %all-gather.9.cloned.1.call-update) | async-done | bytes 3932176 | tf_op jit(solution)/shard_map/all_gather | solution.py:195
  427.6 23.8 %fusion.51 = (f32[768]{0:T(1024)S(1)}, bf16[2560,768]{1,0:T(8,128)(2,1)S(1)}, f32[2560,768]{1,0:T(8,128)}) fusion(f32[2560,768]{1,0:T(8,128)} %fusion.59, f32[768]{0:T(1024)S(1)} %convert_element_type.88, bf16[2560,768]{1,0:T(8,128)(2,1)} %all-gather.9.cloned.1.call-done, bf16[768,768]{1,0:T(8,128)(2,1)S(1)} %copy-done), kind=kOutput, calls=%fused_computation.106 | convolution fusion | flops 3165388032 | bytes 24778752 | tf_op jit(solution)/shard_map/rd,fd->rf/dot_general | solution.py:100
  453.3 5.4 fusion.29
  459.2 8.0 multiply_convert_fusion
  469.2 4.7 convolution_convert_fusion
  473.9 119.7 %reduce-scatter.9.cloned.1.call-done = f32[640,768]{1,0:T(8,128)} async-done(((f32[2560,768]{1,0:T(8,128)}), f32[640,768]{1,0:T(8,128)}) %reduce-scatter.9.cloned.1.call-update) | async-done | bytes 1966096 | tf_op jit(solution)/shard_map/reduce_scatter | solution.py:199
  596.0 73.1 %reduce-scatter.7.cloned.1.call-done = bf16[640,768]{1,0:T(8,128)(2,1)} async-done(((bf16[2560,768]{1,0:T(8,128)(2,1)}), bf16[640,768]{1,0:T(8,128)(2,1)}) %reduce-scatter.7.cloned.1.call-update) | async-done | bytes 983056 | tf_op jit(solution)/shard_map/reduce_scatter | solution.py:187
  675.4 76.9 %all-gather.11.cloned.1.call-done = bf16[2560,768]{1,0:T(8,128)(2,1)} async-done(((bf16[640,768]{1,0:T(8,128)(2,1)}), bf16[2560,768]{1,0:T(8,128)(2,1)}) %all-gather.11.cloned.1.call-update) | async-done | bytes 3932176 | tf_op jit(solution)/shard_map/all_gather | solution.py:209
  752.2 4.5 convolution_convert_fusion.1
  760.0 7.1 multiply_reduce_fusion
  800.9 4.7 bitcast_convert_fusion
  806.0 8.1 fusion.27
  814.2 4.8 fusion.61
  829.5 14.4 %all-reduce.1 = (f32[2,192]{1,0:T(2,128)}, f32[768]{0:T(1024)}) all-reduce(f32[2,192]{1,0:T(2,128)S(1)} %pad_maximum_fusion, f32[768]{0:T(1024)S(1)} %get-tuple-element.37), channel_id=1, replica_groups=mesh['dp'=8,'tensor'=4] {'dp'}, use_global_device_ids=true, to_apply=%region_22.23 | all-reduce | flops 1152 | bytes 9216 | tf_op jit(solution)/shard_map/psum | solution.py:249
  843.9 33.2 %reduce-scatter.11.cloned.1.call-done = bf16[640,768]{1,0:T(8,128)(2,1)} async-done(((bf16[2560,768]{1,0:T(8,128)(2,1)}), bf16[640,768]{1,0:T(8,128)(2,1)}) %reduce-scatter.11.cloned.1.call-update) | async-done | bytes 983056 | tf_op jit(solution)/shard_map/reduce_scatter | solution.py:223
  883.8 41.7 %all-reduce = (f32[768]{0:T(1024)}, f32[768]{0:T(1024)}, f32[768]{0:T(1024)}, f32[768]{0:T(1024)}, f32[768]{0:T(1024)}, /*index=5*/f32[768]{0:T(1024)}) all-reduce(f32[768]{0:T(1024)S(1)} %get-tuple-element.16, f32[768]{0:T(1024)S(1)} %get-tuple-element.21, ...), channel_id=1, replica_groups=mesh['dp'=8,'tensor'=4] {'dp','tensor'}, use_global_device_ids=true, to_apply=%region_16.17 | all-reduce | flops 4608 | bytes 36864 | tf_op jit(solution)/shard_map/psum | solution.py:237
  925.4 71.1 %all-reduce.5.cloned.1.call-done = (f32[768,3,192]{0,2,1:T(8,128)}, f32[192,768]{1,0:T(8,128)}, f32[768,768]{1,0:T(8,128)}, f32[768,768]{1,0:T(8,128)}) async-done(((f32[768,3,192]{0,2,1:T(8,128)}, f32[192,768]{1,0:T(8,128)}, f32[768,768]{1,0:T(8,128)}, f32[768,768]{1,0:T(8,128)}), (f32[768,3,192]{0,2,1:T(8,128)}, f32[192,768]{1,0:T(8,128)}, f32[768,768]{1,0:T(8,128)}, ...) | async-done | bytes 7077904 | tf_op jit(solution)/shard_map/psum | solution.py:249
  (172 shorter events, 112.8 us)
Async XLA Ops:
  7.2 420.5 %copy-start = (bf16[768,768]{1,0:T(8,128)(2,1)S(1)}, bf16[768,768]{1,0:T(8,128)(2,1)}, u32[]{:S(2)}) copy-start(bf16[768,768]{1,0:T(8,128)(2,1)} %param.27) | copy-start | bytes 3538948
  7.2 86.3 %copy-start.44 = (bf16[768,3,192]{0,2,1:T(8,128)(2,1)S(1)}, bf16[768,3,192]{0,2,1:T(8,128)(2,1)}, u32[]{:S(2)}) copy-start(bf16[768,3,192]{0,2,1:T(8,128)(2,1)} %param.19) | copy-start | bytes 2654212
  7.2 86.3 %all-gather.5.cloned.1.call-start = ((), (), s32[]{:S(2)}) async-start(), calls=%async_computation.4 | async-start | bytes 4915200 | tf_op jit(solution)/shard_map/all_gather | solution.py:165
  14.3 255.9 %reduce-scatter.5.cloned.1.call-start = ((), (), s32[]{:S(2)}) async-start(), calls=%async_computation.5 | async-start | bytes 9830400 | tf_op jit(solution)/shard_map/reduce_scatter | solution.py:173
  104.7 8.9 copy-start.7
  135.2 135.0 %copy-start.35 = (f32[768]{0:T(1024)S(1)}, f32[768]{0:T(1024)}, u32[]{:S(2)}) copy-start(f32[768]{0:T(1024)} %param.22) | copy-start | bytes 9220
  135.2 137.5 %copy-start.34 = (f32[768]{0:T(1024)S(1)}, f32[768]{0:T(1024)}, u32[]{:S(2)}) copy-start(f32[768]{0:T(1024)} %param.23) | copy-start | bytes 9220
  135.2 137.5 %copy-start.36 = (f32[768]{0:T(1024)S(1)}, f32[768]{0:T(1024)}, u32[]{:S(2)}) copy-start(f32[768]{0:T(1024)} %param.24) | copy-start | bytes 9220
  135.3 215.9 %all-gather.7.cloned.1.call-start = ((), (), s32[]{:S(2)}) async-start(), calls=%async_computation.6 | async-start | bytes 4915200 | tf_op jit(solution)/shard_map/all_gather | solution.py:182
  274.1 153.6 %all-gather.9.cloned.1.call-start = ((), (), s32[]{:S(2)}) async-start(), calls=%async_computation.8 | async-start | bytes 4915200 | tf_op jit(solution)/shard_map/all_gather | solution.py:195
  274.6 319.0 %reduce-scatter.9.cloned.1.call-start = ((), (), s32[]{:S(2)}) async-start(), calls=%async_computation.9 | async-start | bytes 9830400 | tf_op jit(solution)/shard_map/reduce_scatter | solution.py:199
  427.6 25.7 %copy-start.43 = (bf16[768,768]{1,0:T(8,128)(2,1)S(1)}, bf16[768,768]{1,0:T(8,128)(2,1)}, u32[]{:S(2)}) copy-start(bf16[768,768]{1,0:T(8,128)(2,1)} %param.25) | copy-start | bytes 3538948
  458.7 210.3 %reduce-scatter.7.cloned.1.call-start = ((), (), s32[]{:S(2)}) async-start(), calls=%async_computation.7 | async-start | bytes 4915200 | tf_op jit(solution)/shard_map/reduce_scatter | solution.py:187
  473.8 195.2 %copy-start.37 = (f32[768]{0:T(1024)S(1)}, f32[768]{0:T(1024)}, u32[]{:S(2)}) copy-start(f32[768]{0:T(1024)} %param.28) | copy-start | bytes 9220
  473.9 278.3 %all-gather.11.cloned.1.call-start = ((), (), s32[]{:S(2)}) async-start(), calls=%async_computation.10 | async-start | bytes 4915200 | tf_op jit(solution)/shard_map/all_gather | solution.py:209
  675.3 201.8 %reduce-scatter.11.cloned.1.call-start = ((), (), s32[]{:S(2)}) async-start(), calls=%async_computation.11 | async-start | bytes 4915200 | tf_op jit(solution)/shard_map/reduce_scatter | solution.py:223
  805.7 190.8 %all-reduce.5.cloned.1.call-start = ((), (), s32[]{:S(2)}) async-start(), calls=%async_computation.12 | async-start | bytes 14155776 | tf_op jit(solution)/shard_map/psum | solution.py:249
  806.0 8.2 copy-start.16
  824.6 52.5 %copy-start.3 = (bf16[640,768]{1,0:T(8,128)(2,1)S(1)}, bf16[640,768]{1,0:T(8,128)(2,1)}, u32[]{:S(2)}) copy-start(bf16[640,768]{1,0:T(8,128)(2,1)} %param.15) | copy-start | bytes 2949124
  824.6 52.5 %copy-start.28 = (f32[640]{0:T(1024)S(1)}, f32[640]{0:T(1024)}, u32[]{:S(2)}) copy-start(f32[640]{0:T(1024)} %copy-done.27) | copy-start | bytes 7684
  824.6 52.5 %copy-start.29 = (f32[768]{0:T(1024)S(1)}, f32[768]{0:T(1024)}, u32[]{:S(2)}) copy-start(f32[768]{0:T(1024)} %param.17) | copy-start | bytes 9220
  826.9 52.3 %copy-start.33 = (f32[640]{0:T(1024)S(1)}, f32[640]{0:T(1024)}, u32[]{:S(2)}) copy-start(f32[640]{0:T(1024)} %copy-done.32) | copy-start | bytes 7684
  826.9 52.3 %copy-start.31 = (f32[640]{0:T(1024)S(1)}, f32[640]{0:T(1024)}, u32[]{:S(2)}) copy-start(f32[640]{0:T(1024)} %copy-done.30) | copy-start | bytes 7684
  827.0 54.6 %copy-start.13 = (bf16[640,768]{1,0:T(8,128)(2,1)S(1)}, bf16[640,768]{1,0:T(8,128)(2,1)}, u32[]{:S(2)}) copy-start(bf16[640,768]{1,0:T(8,128)(2,1)} %param.29) | copy-start | bytes 2949124
  (32 other events, 121.6 us)
Sparse Core Ops, SparseCore 0:
  14.4 79.1 all-gather.4
  135.4 134.8 reduce-scatter.4
  274.2 76.9 all-gather.6
  352.6 74.9 all-gather.8
  458.8 134.8 reduce-scatter.8
  595.8 73.1 reduce-scatter.6
  675.4 76.7 all-gather.10
  805.8 71.2 reduce-scatter.10
  881.9 114.5 all-reduce.4
where the time goes:
time: 1010 us
  waiting for transfers between devices  732 us (72%)
  matrix products  105 us (10%)
  local copies, waits for them, and re-layouts  62.3 us (6%)
  blocking collectives  56.1 us (6%)
  other arithmetic  38.2 us (4%)
  between operations  14.8 us (1%)
    reduce_scatter x1, waiting for transfers between devices, local(): lax.psum_scatter(jnp.dot(blend_low, mixer_weight, preferred_element_type=...  135 us
    reduce_scatter x1, waiting for transfers between devices, local(): lax.psum_scatter(jnp.einsum('rf,df->rd', grad_pre_low, up_weight, preferr...  120 us
    all_gather x1, waiting for transfers between devices, local(): whole_one = lax.all_gather(low_one, 'tensor', axis=0, tiled=True)  79 us
    all_gather x1, waiting for transfers between devices, local(): lax.all_gather(grad_first.astype(jnp.bfloat16), 'tensor', axis=0, tiled=T...  76.9 us
    all_gather x1, waiting for transfers between devices, local(): whole_two = lax.all_gather(low_two, 'tensor', axis=0, tiled=True)  76.5 us
    reduce_scatter x1, waiting for transfers between devices, local(): lax.psum_scatter(jnp.dot(active, down_weight, preferred_element_type=jnp....  73.1 us
    psum x1, waiting for transfers between devices, local(): lax.psum((weight_terms[0], weight_terms[1], weight_terms[2], weight_terms...  71.1 us
    all_gather x1, waiting for transfers between devices, local(): whole_grad = lax.all_gather(output_grad, 'tensor', axis=0, tiled=True)  67.5 us
  transfers between devices with their start and end apart: 9, of which 9 were waited for; matrix products, arithmetic and copies ran while one was open for 5% of the time, Pallas kernels for 0%

commit v1 on v0

--- a/solution.py
+++ b/solution.py
@@ -6,6 +6,11 @@
 HD = 64
 SLOTS = 80
 masked_score = -1000000000.0
+
+
+def pieces_all_rest(local_x, bus_axis, mesh_name="dp"):
+    h_now = lax.psum(local_x, bus_axis)
+    return lax.psum(h_now, mesh_name)
 
 
 def layer_norm(inputs, norm_gain, norm_shift):
@@ -234,7 +239,7 @@
     )
     grad_tokens = grad_first + grad_inputs
     sum_gain_one, sum_shift_one, sum_mix_bias, sum_gain_two, sum_shift_two, sum_down_bias = (
-        lax.psum(
+        pieces_all_rest(
             (
                 grad_gain_one,
                 grad_shift_one,
@@ -243,7 +248,7 @@
                 grad_shift_two,
                 jnp.sum(grad_output, axis=0),
             ),
-            ("dp", "tensor"),
+            "tensor",
         )
     )
     sum_weight_in, sum_bias_in, sum_mix, sum_up, sum_up_b, sum_down = lax.psum(

time: 1010 us -> 1010 us (level)
  waiting for transfers between devices: 732 us -> 746 us
  blocking collectives: 56.1 us -> 42.3 us
    reduce_scatter x1, waiting for transfers between devices: 33.2 us -> 47.6 us  [local(): lax.psum_scatter(jnp.einsum('rjc,djc->rd', grad_projected, input_weight,...]
    psum x2, blocking collectives: 56.1 us -> 42.3 us  [the longest x1 24.3 us: pieces_all_rest(): return lax.psum(h_now, mesh_name)]
where the time goes in v1:
time: 1010 us
  waiting for transfers between devices  746 us (74%)
  matrix products  105 us (10%)
  local copies, waits for them, and re-layouts  62.3 us (6%)
  blocking collectives  42.3 us (4%)
  other arithmetic  38.2 us (4%)
  between operations  14.8 us (1%)
    reduce_scatter x1, waiting for transfers between devices, local(): lax.psum_scatter(jnp.dot(blend_low, mixer_weight, preferred_element_type=...  135 us
    reduce_scatter x1, waiting for transfers between devices, local(): lax.psum_scatter(jnp.einsum('rf,df->rd', grad_pre_low, up_weight, preferr...  120 us
    all_gather x1, waiting for transfers between devices, local(): whole_one = lax.all_gather(low_one, 'tensor', axis=0, tiled=True)  79 us
    all_gather x1, waiting for transfers between devices, local(): lax.all_gather(grad_first.astype(jnp.bfloat16), 'tensor', axis=0, tiled=T...  76.8 us
    all_gather x1, waiting for transfers between devices, local(): whole_two = lax.all_gather(low_two, 'tensor', axis=0, tiled=True)  76.5 us
    reduce_scatter x1, waiting for transfers between devices, local(): lax.psum_scatter(jnp.dot(active, down_weight, preferred_element_type=jnp....  73.1 us
    psum x1, waiting for transfers between devices, local(): lax.psum((weight_terms[0], weight_terms[1], weight_terms[2], weight_terms...  70.1 us
    all_gather x1, waiting for transfers between devices, local(): whole_grad = lax.all_gather(output_grad, 'tensor', axis=0, tiled=True)  67.5 us
  transfers between devices with their start and end apart: 9, of which 9 were waited for; matrix products, arithmetic and copies ran while one was open for 5% of the time, Pallas kernels for 0%

profile of v1, /device:TPU:0, one launch (start us, length us, event | category | flops | bytes accessed | tf_op | source)
XLA Modules:
  0.0 1009.7 jit_solution(15641046415969071522)
XLA Ops:
  14.6 79.0 %all-gather.5.cloned.1.call-done = bf16[2560,768]{1,0:T(8,128)(2,1)} async-done(((bf16[640,768]{1,0:T(8,128)(2,1)}), bf16[2560,768]{1,0:T(8,128)(2,1)}) %all-gather.5.cloned.1.call-update) | async-done | bytes 3932176 | tf_op jit(solution)/shard_map/all_gather | solution.py:170
  93.6 4.6 fusion.6
  104.7 4.7 squeeze.4
  113.5 5.2 fusion.57
  135.3 134.9 %reduce-scatter.5.cloned.1.call-done = f32[640,768]{1,0:T(8,128)} async-done(((f32[2560,768]{1,0:T(8,128)}), f32[640,768]{1,0:T(8,128)}) %reduce-scatter.5.cloned.1.call-update) | async-done | bytes 1966096 | tf_op jit(solution)/shard_map/reduce_scatter | solution.py:178
  274.7 76.5 %all-gather.7.cloned.1.call-done = bf16[2560,768]{1,0:T(8,128)(2,1)} async-done(((bf16[640,768]{1,0:T(8,128)(2,1)}), bf16[2560,768]{1,0:T(8,128)(2,1)}) %all-gather.7.cloned.1.call-update) | async-done | bytes 3932176 | tf_op jit(solution)/shard_map/all_gather | solution.py:187
  351.2 9.0 fusion.59
  360.2 67.5 %all-gather.9.cloned.1.call-done = bf16[2560,768]{1,0:T(8,128)(2,1)} async-done(((bf16[640,768]{1,0:T(8,128)(2,1)}), bf16[2560,768]{1,0:T(8,128)(2,1)}) %all-gather.9.cloned.1.call-update) | async-done | bytes 3932176 | tf_op jit(solution)/shard_map/all_gather | solution.py:200
  427.6 23.8 %fusion.51 = (f32[768]{0:T(1024)S(1)}, bf16[2560,768]{1,0:T(8,128)(2,1)S(1)}, f32[2560,768]{1,0:T(8,128)}) fusion(f32[2560,768]{1,0:T(8,128)} %fusion.59, f32[768]{0:T(1024)S(1)} %convert_element_type.88, bf16[2560,768]{1,0:T(8,128)(2,1)} %all-gather.9.cloned.1.call-done, bf16[768,768]{1,0:T(8,128)(2,1)S(1)} %copy-done), kind=kOutput, calls=%fused_computation.106 | convolution fusion | flops 3165388032 | bytes 24778752 | tf_op jit(solution)/shard_map/rd,fd->rf/dot_general | solution.py:105
  453.3 5.4 fusion.29
  459.2 8.0 multiply_convert_fusion
  469.1 4.7 convolution_convert_fusion
  473.9 119.8 %reduce-scatter.9.cloned.1.call-done = f32[640,768]{1,0:T(8,128)} async-done(((f32[2560,768]{1,0:T(8,128)}), f32[640,768]{1,0:T(8,128)}) %reduce-scatter.9.cloned.1.call-update) | async-done | bytes 1966096 | tf_op jit(solution)/shard_map/reduce_scatter | solution.py:204
  596.0 73.1 %reduce-scatter.7.cloned.1.call-done = bf16[640,768]{1,0:T(8,128)(2,1)} async-done(((bf16[2560,768]{1,0:T(8,128)(2,1)}), bf16[640,768]{1,0:T(8,128)(2,1)}) %reduce-scatter.7.cloned.1.call-update) | async-done | bytes 983056 | tf_op jit(solution)/shard_map/reduce_scatter | solution.py:192
  675.4 76.8 %all-gather.11.cloned.1.call-done = bf16[2560,768]{1,0:T(8,128)(2,1)} async-done(((bf16[640,768]{1,0:T(8,128)(2,1)}), bf16[2560,768]{1,0:T(8,128)(2,1)}) %all-gather.11.cloned.1.call-update) | async-done | bytes 3932176 | tf_op jit(solution)/shard_map/all_gather | solution.py:214
  752.2 4.5 convolution_convert_fusion.1
  760.0 7.1 multiply_reduce_fusion
  800.9 4.7 bitcast_convert_fusion
  806.0 8.1 fusion.27
  814.2 4.8 fusion.61
  829.5 47.6 %reduce-scatter.11.cloned.1.call-done = bf16[640,768]{1,0:T(8,128)(2,1)} async-done(((bf16[2560,768]{1,0:T(8,128)(2,1)}), bf16[640,768]{1,0:T(8,128)(2,1)}) %reduce-scatter.11.cloned.1.call-update) | async-done | bytes 983056 | tf_op jit(solution)/shard_map/reduce_scatter | solution.py:228
  883.8 18.0 %all-reduce.2 = (f32[768]{0:T(1024)S(1)}, f32[768]{0:T(1024)S(1)}, f32[768]{0:T(1024)S(1)}, f32[768]{0:T(1024)S(1)}, f32[768]{0:T(1024)S(1)}, /*index=5*/f32[768]{0:T(1024)S(1)}) all-reduce(f32[768]{0:T(1024)S(1)} %get-tuple-element.16, f32[768]{0:T(1024)S(1)} %get-tuple-element.21, ...), channel_id=1, replica_groups=mesh['dp'=8,'tensor'=4] {'tensor'}, use_global_device_ids=true, to_apply=%region_16.17 | all-reduce | flops 4608 | bytes 36864 | tf_op jit(solution)/shard_map/psum | solution.py:12
  901.8 24.3 %all-reduce = (f32[768]{0:T(1024)}, f32[768]{0:T(1024)}, f32[2,192]{1,0:T(2,128)}, f32[768]{0:T(1024)}, f32[768]{0:T(1024)}, /*index=5*/f32[768]{0:T(1024)}, f32[768]{0:T(1024)}, f32[768]{0:T(1024)}) all-reduce(f32[768]{0:T(1024)S(1)} %get-tuple-element.37, ...), channel_id=1, replica_groups=mesh['dp'=8,'tensor'=4] {'dp'}, use_global_device_ids=true, to_apply=%region_17.18 | all-reduce | flops 5760 | bytes 46080 | tf_op jit(solution)/shard_map/psum | solution.py:13
  926.1 70.1 %all-reduce.5.cloned.1.call-done = (f32[768,3,192]{0,2,1:T(8,128)}, f32[192,768]{1,0:T(8,128)}, f32[768,768]{1,0:T(8,128)}, f32[768,768]{1,0:T(8,128)}) async-done(((f32[768,3,192]{0,2,1:T(8,128)}, f32[192,768]{1,0:T(8,128)}, f32[768,768]{1,0:T(8,128)}, f32[768,768]{1,0:T(8,128)}), (f32[768,3,192]{0,2,1:T(8,128)}, f32[192,768]{1,0:T(8,128)}, f32[768,768]{1,0:T(8,128)}, ...) | async-done | bytes 7077904 | tf_op jit(solution)/shard_map/psum | solution.py:254
  (172 shorter events, 112.8 us)
Async XLA Ops:
  7.2 420.5 %copy-start = (bf16[768,768]{1,0:T(8,128)(2,1)S(1)}, bf16[768,768]{1,0:T(8,128)(2,1)}, u32[]{:S(2)}) copy-start(bf16[768,768]{1,0:T(8,128)(2,1)} %param.27) | copy-start | bytes 3538948
  7.2 86.3 %copy-start.44 = (bf16[768,3,192]{0,2,1:T(8,128)(2,1)S(1)}, bf16[768,3,192]{0,2,1:T(8,128)(2,1)}, u32[]{:S(2)}) copy-start(bf16[768,3,192]{0,2,1:T(8,128)(2,1)} %param.19) | copy-start | bytes 2654212
  7.2 86.3 %all-gather.5.cloned.1.call-start = ((), (), s32[]{:S(2)}) async-start(), calls=%async_computation.4 | async-start | bytes 4915200 | tf_op jit(solution)/shard_map/all_gather | solution.py:170
  14.3 255.9 %reduce-scatter.5.cloned.1.call-start = ((), (), s32[]{:S(2)}) async-start(), calls=%async_computation.5 | async-start | bytes 9830400 | tf_op jit(solution)/shard_map/reduce_scatter | solution.py:178
  104.7 8.9 copy-start.7
  135.2 135.0 %copy-start.35 = (f32[768]{0:T(1024)S(1)}, f32[768]{0:T(1024)}, u32[]{:S(2)}) copy-start(f32[768]{0:T(1024)} %param.22) | copy-start | bytes 9220
  135.2 137.5 %copy-start.34 = (f32[768]{0:T(1024)S(1)}, f32[768]{0:T(1024)}, u32[]{:S(2)}) copy-start(f32[768]{0:T(1024)} %param.23) | copy-start | bytes 9220
  135.2 137.5 %copy-start.36 = (f32[768]{0:T(1024)S(1)}, f32[768]{0:T(1024)}, u32[]{:S(2)}) copy-start(f32[768]{0:T(1024)} %param.24) | copy-start | bytes 9220
  135.3 215.9 %all-gather.7.cloned.1.call-start = ((), (), s32[]{:S(2)}) async-start(), calls=%async_computation.6 | async-start | bytes 4915200 | tf_op jit(solution)/shard_map/all_gather | solution.py:187
  274.1 153.6 %all-gather.9.cloned.1.call-start = ((), (), s32[]{:S(2)}) async-start(), calls=%async_computation.8 | async-start | bytes 4915200 | tf_op jit(solution)/shard_map/all_gather | solution.py:200
  274.6 319.0 %reduce-scatter.9.cloned.1.call-start = ((), (), s32[]{:S(2)}) async-start(), calls=%async_computation.9 | async-start | bytes 9830400 | tf_op jit(solution)/shard_map/reduce_scatter | solution.py:204
  427.6 25.7 %copy-start.43 = (bf16[768,768]{1,0:T(8,128)(2,1)S(1)}, bf16[768,768]{1,0:T(8,128)(2,1)}, u32[]{:S(2)}) copy-start(bf16[768,768]{1,0:T(8,128)(2,1)} %param.25) | copy-start | bytes 3538948
  458.7 210.4 %reduce-scatter.7.cloned.1.call-start = ((), (), s32[]{:S(2)}) async-start(), calls=%async_computation.7 | async-start | bytes 4915200 | tf_op jit(solution)/shard_map/reduce_scatter | solution.py:192
  473.8 195.2 %copy-start.37 = (f32[768]{0:T(1024)S(1)}, f32[768]{0:T(1024)}, u32[]{:S(2)}) copy-start(f32[768]{0:T(1024)} %param.28) | copy-start | bytes 9220
  473.9 278.3 %all-gather.11.cloned.1.call-start = ((), (), s32[]{:S(2)}) async-start(), calls=%async_computation.10 | async-start | bytes 4915200 | tf_op jit(solution)/shard_map/all_gather | solution.py:214
  675.3 201.8 %reduce-scatter.11.cloned.1.call-start = ((), (), s32[]{:S(2)}) async-start(), calls=%async_computation.11 | async-start | bytes 4915200 | tf_op jit(solution)/shard_map/reduce_scatter | solution.py:228
  805.7 190.4 %all-reduce.5.cloned.1.call-start = ((), (), s32[]{:S(2)}) async-start(), calls=%async_computation.12 | async-start | bytes 14155776 | tf_op jit(solution)/shard_map/psum | solution.py:254
  806.0 8.2 copy-start.16
  824.6 52.5 %copy-start.3 = (bf16[640,768]{1,0:T(8,128)(2,1)S(1)}, bf16[640,768]{1,0:T(8,128)(2,1)}, u32[]{:S(2)}) copy-start(bf16[640,768]{1,0:T(8,128)(2,1)} %param.15) | copy-start | bytes 2949124
  824.6 52.5 %copy-start.28 = (f32[640]{0:T(1024)S(1)}, f32[640]{0:T(1024)}, u32[]{:S(2)}) copy-start(f32[640]{0:T(1024)} %copy-done.27) | copy-start | bytes 7684
  824.6 52.5 %copy-start.29 = (f32[768]{0:T(1024)S(1)}, f32[768]{0:T(1024)}, u32[]{:S(2)}) copy-start(f32[768]{0:T(1024)} %param.17) | copy-start | bytes 9220
  826.9 52.3 %copy-start.33 = (f32[640]{0:T(1024)S(1)}, f32[640]{0:T(1024)}, u32[]{:S(2)}) copy-start(f32[640]{0:T(1024)} %copy-done.32) | copy-start | bytes 7684
  826.9 52.3 %copy-start.31 = (f32[640]{0:T(1024)S(1)}, f32[640]{0:T(1024)}, u32[]{:S(2)}) copy-start(f32[640]{0:T(1024)} %copy-done.30) | copy-start | bytes 7684
  827.0 54.6 %copy-start.13 = (bf16[640,768]{1,0:T(8,128)(2,1)S(1)}, bf16[640,768]{1,0:T(8,128)(2,1)}, u32[]{:S(2)}) copy-start(bf16[640,768]{1,0:T(8,128)(2,1)} %param.29) | copy-start | bytes 2949124
  (32 other events, 121.6 us)
Sparse Core Ops, SparseCore 0:
  14.4 79.1 all-gather.4
  135.4 134.8 reduce-scatter.4
  274.2 76.9 all-gather.6
  352.6 74.9 all-gather.8
  458.8 134.8 reduce-scatter.8
  595.8 73.1 reduce-scatter.6
  675.4 76.7 all-gather.10
  805.8 71.2 reduce-scatter.10
  881.9 114.1 all-reduce.4
